TPU v7x, 32 devices: a whole 2x2x4 slice. The times are simulated.
32 devices in a mesh: group: 2 (over x), wide: 16 (over z, y, core).
Axes of the slice: x: 2, y: 2, z: 4, core: 2. Of those that a mesh axis runs over, the one named last changes fastest.
Arguments:
- tokens: bfloat16 [192, 2688], P('group', 'wide'), parts along dimension 0, may hold values from -6 to 6
- mix_gain: bfloat16 [2688], replicated, may hold values from 0.099609375 to 1.8984375
- proj_inner: bfloat16 [2688, 2, 4096], P(None, None, 'wide'), may hold values from -0.125 to 0.125
- proj_maps: bfloat16 [2688, 2048], P(None, 'wide'), may hold values from -0.125 to 0.125
- proj_step: bfloat16 [2688, 64], P(None, 'wide'), may hold values from -0.125 to 0.125
- window_inner: bfloat16 [192, 3, 4096], P('group', None, 'wide'), parts along dimension 0, may hold values from -6 to 6
- window_maps: bfloat16 [192, 3, 2048], P('group', None, 'wide'), parts along dimension 0, may hold values from -6 to 6
- kernel_inner: bfloat16 [4, 4096], P(None, 'wide'), may hold values from -3 to 3
- kernel_maps: bfloat16 [4, 2048], P(None, 'wide'), may hold values from -3 to 3
- step_bias: float32 [64], P('wide'), may hold values from -4 to -1
- decay_log: float32 [64], P('wide'), may hold values from -1 to 2.5
- skip_gain: float32 [64], P('wide'), may hold values from 0.5 to 2
- gated_gain: bfloat16 [4096], P('wide'), may hold values from 0.099609375 to 1.8984375
- proj_out: bfloat16 [4096, 2688], P('wide'), may hold values from -0.125 to 0.125
- ssm_state: float32 [192, 64, 64, 128], P('group', 'wide'), parts along dimension 0, may hold values from -0.6 to 0.6
- moe_gain: bfloat16 [2688], replicated, may hold values from 0.099609375 to 1.8984375
- router_weight: bfloat16 [2688, 16], replicated, may hold values from -0.125 to 0.125
- expert_ids: int32 [192, 6], P('group'), parts along dimension 0, may hold values from 0 to 15, all different within a row; in each aligned block of 96 rows (0 to 95, 96 to 191, ...) at most 96 rows name the same one
- expert_up: bfloat16 [16, 2688, 928], P('wide'), may hold values from -0.125 to 0.125
- expert_down: bfloat16 [16, 928, 2688], P('wide'), may hold values from -0.1875 to 0.1875
Outputs:
- next_hidden: bfloat16 [192, 2688], P('group', 'wide'), parts along dimension 0
- new_state: float32 [192, 64, 64, 128], P('group', 'wide'), parts along dimension 0
There are 2 independent parts, one for each index of `group`. A program takes and returns all parts, laid end to end along the dimension named above; an argument that names none is the same for every part. Nothing has to cross between parts.
Inputs may be any that keep to these rules, and one draw needn't show every extreme that they name: `expert_ids`: each token names 6 different experts; no expert is named by more than 96 tokens of a part, a bound that some block reaches.
All inputs are finite; a program needn't handle non-finite values.
Results may differ from a plain program's by a relative error of at most 0.013.
Values may be sent and summed in bfloat16 or wider, within the bound.
A program may use at most 128 MiB of HBM per device.

v0:
```python
import jax
import jax.numpy as jnp
from jax import lax
from jax.sharding import PartitionSpec as P

WIDTH = 2688
HEADS = 64
HEAD_DIM = 64
STATE = 128
GROUPS = 8
TOPK = 6
INNER = 4096
epsilon = 1e-05


def rms_scale(values, axis):
    return lax.rsqrt(jnp.mean(values * values, axis=axis, keepdims=True) + epsilon)


def convolve(window, fresh, kernel):
    stacked = jnp.concatenate([window, fresh[:, None, :]], axis=1).astype(jnp.float32)
    mixed = jnp.sum(stacked * kernel.astype(jnp.float32)[None], axis=1)
    return jax.nn.silu(mixed).astype(jnp.bfloat16)


def expert_rows(rows, upward, downward):
    hidden_units = jnp.dot(rows, upward, preferred_element_type=jnp.float32)
    active = jnp.square(jnp.maximum(hidden_units, 0.0)).astype(jnp.bfloat16)
    return jnp.dot(active, downward, preferred_element_type=jnp.float32).astype(jnp.bfloat16)


def route_gates(logits, expert_ids):
    onehot = (
        expert_ids[:, :, None] == jnp.arange(logits.shape[1], dtype=jnp.int32)[None, None, :]
    ).astype(jnp.float32)
    chosen = jnp.sum(onehot * logits[:, None, :], axis=2)
    score = jax.nn.sigmoid(chosen)
    return score / jnp.sum(score, axis=1, keepdims=True)


def slot_codes(expert_ids, experts, capacity):
    flat = expert_ids.reshape(-1)
    onehot = (flat[:, None] == jnp.arange(experts, dtype=jnp.int32)[None, :]).astype(jnp.int32)
    before = jnp.cumsum(onehot, axis=0) - onehot
    slots = jnp.sum(before * onehot, axis=1)
    return (flat * capacity + slots).reshape(expert_ids.shape)


def slot_tables(codes, gates, count):
    targets = jnp.arange(count, dtype=jnp.int32)
    match = codes[None, :, :] == targets[:, None, None]
    pick = jnp.any(match, axis=2).astype(jnp.bfloat16)
    weigh = jnp.sum(jnp.where(match, gates[None], 0.0), axis=2)
    return (pick, weigh)


def local(
    tokens,
    mix_gain,
    proj_inner,
    proj_maps,
    proj_step,
    window_inner,
    window_maps,
    kernel_inner,
    kernel_maps,
    step_bias,
    decay_log,
    skip_gain,
    gated_gain,
    proj_out,
    ssm_state,
    moe_gain,
    router_weight,
    expert_ids,
    expert_up,
    expert_down,
):
    devices = lax.axis_size("wide")
    device = lax.axis_index("wide")
    seqs = tokens.shape[0]
    slice_width = tokens.shape[1]
    capacity = min(seqs, 4 * seqs * TOPK // devices)
    full_tokens = lax.all_gather(tokens, "wide", axis=1, tiled=True)
    tokens_float = full_tokens.astype(jnp.float32)
    normed = (tokens_float * rms_scale(tokens_float, 1) * mix_gain.astype(jnp.float32)).astype(
        jnp.bfloat16
    )
    local_inner = proj_inner.shape[2]
    inner = jnp.dot(
        normed, proj_inner.reshape(WIDTH, 2 * local_inner), preferred_element_type=jnp.float32
    ).astype(jnp.bfloat16)
    gate_input = inner[:, :local_inner]
    raw_inner = inner[:, local_inner:]
    maps_raw = jnp.dot(normed, proj_maps, preferred_element_type=jnp.float32).astype(jnp.bfloat16)
    step_raw = jnp.dot(normed, proj_step, preferred_element_type=jnp.float32).astype(jnp.bfloat16)
    conv_inner = convolve(window_inner, raw_inner, kernel_inner)
    conv_maps = convolve(window_maps, maps_raw, kernel_maps)
    all_maps = lax.all_gather(conv_maps, "wide", axis=1, tiled=True)
    local_heads = proj_step.shape[1]
    group = device * local_heads // (HEADS // GROUPS)
    in_maps = lax.dynamic_slice_in_dim(all_maps, group * STATE, STATE, 1).astype(jnp.float32)
    out_maps = lax.dynamic_slice_in_dim(all_maps, GROUPS * STATE + group * STATE, STATE, 1).astype(
        jnp.float32
    )
    step_size = jax.nn.softplus(step_raw.astype(jnp.float32) + step_bias)
    decay = jnp.exp(-jnp.exp(decay_log) * step_size)
    head_inputs = conv_inner.astype(jnp.float32).reshape(seqs, local_heads, HEAD_DIM)
    driven = (step_size[:, :, None] * head_inputs)[..., None] * in_maps[:, None, None, :]
    new_state = decay[:, :, None, None] * ssm_state + driven
    readout = (
        jnp.einsum("shpn,sn->shp", new_state, out_maps, precision=lax.Precision.HIGHEST)
        + skip_gain[None, :, None] * head_inputs
    )
    gated = readout.reshape(seqs, local_inner) * jax.nn.silu(gate_input.astype(jnp.float32))
    group_mask = (jnp.arange(GROUPS, dtype=jnp.int32) == group).astype(jnp.float32)
    partial_squares = jnp.sum(gated * gated, axis=1)[:, None] * group_mask[None, :]
    group_squares = lax.psum(partial_squares, "wide")
    own_squares = jnp.sum(group_squares * group_mask[None, :], axis=1, keepdims=True)
    norm_scale = lax.rsqrt(own_squares / (INNER // GROUPS) + epsilon)
    gated_out = (gated * norm_scale * gated_gain.astype(jnp.float32)).astype(jnp.bfloat16)
    mixer_terms = jnp.dot(gated_out, proj_out, preferred_element_type=jnp.float32)
    codes = slot_codes(expert_ids, devices, capacity)
    mixer_slice = lax.psum_scatter(mixer_terms, "wide", scatter_dimension=1, tiled=True)
    hidden_round = (tokens.astype(jnp.float32) + mixer_slice).astype(jnp.bfloat16)
    hidden_slice = lax.optimization_barrier(hidden_round).astype(jnp.float32)
    gain_slice = lax.dynamic_slice_in_dim(moe_gain, device * slice_width, slice_width, 0).astype(
        jnp.float32
    )
    router_slice = lax.dynamic_slice_in_dim(
        router_weight, device * slice_width, slice_width, 0
    ).astype(jnp.float32)
    weighted = hidden_slice * gain_slice
    squares, part_logits = lax.psum(
        (
            jnp.sum(hidden_slice * hidden_slice, axis=1),
            jnp.dot(weighted, router_slice, precision=lax.Precision.HIGHEST),
        ),
        "wide",
    )
    moe_scale = lax.rsqrt(squares[:, None] / WIDTH + epsilon)
    gates = route_gates(part_logits * moe_scale, expert_ids)
    moe_input = (hidden_slice * moe_scale * gain_slice).astype(jnp.bfloat16)
    pick, weigh = slot_tables(codes, gates, devices * capacity)
    sent = (
        jnp.dot(pick, moe_input, preferred_element_type=jnp.float32)
        .astype(jnp.bfloat16)
        .reshape(devices, capacity, slice_width)
    )
    served = expert_rows(
        lax.all_to_all(sent, "wide", split_axis=0, concat_axis=2, tiled=True)[0],
        expert_up[0],
        expert_down[0],
    )
    returned = lax.all_to_all(served[None], "wide", split_axis=2, concat_axis=0, tiled=True)
    moe_slice = jnp.dot(
        weigh.T,
        returned.reshape(devices * capacity, slice_width).astype(jnp.float32),
        precision=lax.Precision.HIGHEST,
    )
    next_hidden = (hidden_slice + moe_slice).astype(jnp.bfloat16)
    return (next_hidden, new_state)


def solution(mesh):
    in_specs = (
        P("group", "wide"),
        P(),
        P(None, None, "wide"),
        P(None, "wide"),
        P(None, "wide"),
        P("group", None, "wide"),
        P("group", None, "wide"),
        P(None, "wide"),
        P(None, "wide"),
        P("wide"),
        P("wide"),
        P("wide"),
        P("wide"),
        P("wide", None),
        P("group", "wide", None, None),
        P(),
        P(),
        P("group", None),
        P("wide", None, None),
        P("wide", None, None),
    )
    out_specs = (P("group", "wide"), P("group", "wide", None, None))
    return jax.shard_map(local, mesh=mesh, in_specs=in_specs, out_specs=out_specs, check_vma=False)
```

profile of v0, /device:TPU:0, one launch (start us, length us, event | category | flops | bytes accessed | tf_op | source)
XLA Modules:
  0.0 292.7 jit_solution(6536486973410003831)
XLA Ops:
  7.2 0.0 copy-start
  7.2 0.0 reduce-scatter.4.cloned.1.call-start
  7.3 0.0 copy-start.2
  7.3 25.6 %all_gather.6 = bf16[96,2688]{0,1:T(8,128)(2,1)S(1)} all-gather(bf16[96,168]{0,1:T(8,128)(2,1)} %param.20), channel_id=1, replica_groups=mesh['group'=2,'wide'=16] {'wide'}, dimensions={1}, use_global_device_ids=true | all-gather | bytes 548352 | tf_op jit(solution)/shard_map/all_gather | solution.py:84
  32.9 0.4 fusion.11
  33.3 0.7 convert_element_type.109
  34.0 0.7 convert_element_type.120
  34.6 1.8 fusion.24
  36.6 18.5 %all_gather.7 = bf16[96,2048]{1,0:T(8,128)(2,1)S(1)} all-gather(bf16[96,128]{1,0:T(8,128)(2,1)S(1)} %multiply_convert_fusion.3), channel_id=1, replica_groups=mesh['group'=2,'wide'=16] {'wide'}, dimensions={1}, use_global_device_ids=true | all-gather | bytes 417792 | tf_op jit(solution)/shard_map/all_gather | solution.py:99
  55.1 0.5 copy.88
  55.5 0.0 copy-start.7
  55.6 0.0 copy-start.4
  55.6 0.0 copy-start.11
  55.6 1.2 convolution_convert_fusion.1
  56.9 0.1 copy.71
  57.0 0.5 multiply_exponential_fusion
  57.6 0.1 convert_multiply_fusion.3
  57.6 0.1 copy.72
  57.8 0.1 copy.70
  57.9 7.0 %multiply_add_fusion = f32[96,4,64,128]{3,2,1,0:T(8,128)S(1)} fusion(f32[96,4,64,128]{3,2,1,0:T(8,128)} %param.34, f32[96,128]{1,0:T(8,128)S(1)} %get-tuple-element.5, f32[96,4,64]{2,1,0:T(4,128)S(1)} %copy.72, f32[96,4]{1,0:T(8,128)S(1)} %copy.70), kind=kLoop, calls=%fused_computation | loop fusion | flops 9437184 | bytes 25314816 | tf_op jit(solution)/shard_map/add | solution.py:110
  64.9 0.0 copy-start.1
  64.9 4.8 %copy-done.1 = f32[96,4,64,128]{3,2,1,0:T(8,128)} copy-done((f32[96,4,64,128]{3,2,1,0:T(8,128)}, f32[96,4,64,128]{3,2,1,0:T(8,128)S(1)}, u32[]{:S(2)}) %copy-start.1) | copy-done | bytes 12582936
  69.7 14.7 %fusion.40 = f32[96,1,4,64]{3,1,2,0:T(1,128)S(1)} fusion(f32[96,4,64,128]{3,2,1,0:T(8,128)S(1)} %multiply_add_fusion, bf16[96,128,1,1]{1,0,2,3:T(8,128)(2,1)S(1)} %get-tuple-element.4), kind=kOutput, calls=%fused_computation.52 | convolution fusion | flops 37748736 | bytes 12705792 | tf_op jit(solution)/shard_map/shpn,sn->shp/dot_general | solution.py:112
  84.4 0.1 copy.84
  84.5 0.0 copy-done.8
  84.5 0.1 fusion.30
  84.6 0.1 copy.73
  84.7 0.1 multiply_reduce_fusion.2
  84.8 0.1 broadcast_multiply_fusion.1
  84.9 31.1 %psum.21 = f32[96,8]{0,1:T(8,128)S(1)} all-reduce(f32[96,8]{0,1:T(8,128)S(1)} %broadcast_multiply_fusion.1), channel_id=1, replica_groups=mesh['group'=2,'wide'=16] {'wide'}, use_global_device_ids=true, to_apply=%region_4.5 | all-reduce | flops 768 | bytes 6144 | tf_op jit(solution)/shard_map/psum | solution.py:118
  116.0 0.1 multiply_reduce_fusion.3
  116.1 1.8 fusion.39
  117.9 0.0 reduce-scatter.4.cloned.1.call-update
  117.9 0.1 copy.74
  118.0 0.1 eq.60
  118.2 1.7 reduce-window.6
  119.9 0.2 slice_reduce_fusion
  120.1 0.1 bitcast_bitcast_fusion
  120.2 0.1 reduce_sum.101
  120.4 0.1 copy.77
  120.4 0.8 dynamic-slice_convert_fusion.1
  121.2 0.6 fusion.4
  121.9 50.8 %reduce-scatter.4.cloned.1.call-done = f32[96,168]{0,1:T(8,128)} async-done(((f32[96,2688]{0,1:T(8,128)}), f32[96,168]{0,1:T(8,128)}) %reduce-scatter.4.cloned.1.call-update) | async-done | bytes 64528
  172.7 0.9 add_convert_fusion
  173.6 0.9 fusion.35
  174.5 30.5 %all-reduce.2 = (f32[96,16]{0,1:T(8,128)S(1)}, f32[96]{0:T(128)S(1)}) all-reduce(f32[96,16]{0,1:T(8,128)S(1)} %fusion.35, f32[96]{0:T(128)S(1)} %fusion.36), channel_id=1, replica_groups=mesh['group'=2,'wide'=16] {'wide'}, use_global_device_ids=true, to_apply=%region_10.11 | all-reduce | flops 1632 | bytes 13056 | tf_op jit(solution)/shard_map/psum | solution.py:134
  205.0 0.3 convolution_convert_fusion
  205.4 0.6 reshape.115
  205.9 0.2 copy.78
  206.1 21.2 %all_to_all.30 = bf16[16,96,168]{1,2,0:T(8,128)(2,1)S(1)} all-to-all(bf16[16,96,168]{1,2,0:T(8,128)(2,1)S(1)} %copy.78), channel_id=1, replica_groups=mesh['group'=2,'wide'=16] {'wide'}, dimensions={0} | all-to-all | bytes 1032192 | tf_op jit(solution)/shard_map/all_to_all | solution.py:151
  227.4 6.5 %fusion.8 = bf16[1,96,2688]{2,1,0:T(8,128)(2,1)S(1)} fusion(bf16[1,928,2688]{2,1,0:T(8,128)(2,1)} %param.39, bf16[96,2688]{0,1:T(8,128)(2,1)S(1)} %bitcast.74, bf16[1,2688,928]{1,2,0:T(8,128)(2,1)} %param.38), kind=kOutput, calls=%fused_computation.9 | convolution fusion | flops 958399488 | bytes 11010048 | tf_op jit(solution)/shard_map/dot_general | solution.py:29
  233.9 1.9 copy.80
  235.8 0.5 broadcast.123
  236.3 14.9 %reduce.2 = bf16[2688,96]{1,0:T(8,128)(2,1)S(1)} reduce(bf16[2688,1,96]{2,1,0:T(2,128)(2,1)S(1)} %bitcast.70, bf16[]{:T(256)} %broadcast.123), dimensions={1}, to_apply=%bitcast.55.reduce_sub_computation | reduce | bytes 1032194
  251.3 1.9 reshape.122
  253.2 4.5 %all-to-all-start.1 = ((bf16[16,2,8064]{2,1,0:T(2,128)(2,1)}), bf16[16,2,8064]{2,1,0:T(2,128)(2,1)}, u32[]{:S(2)}, u32[]{:S(2)}) async-start(bf16[16,2,8064]{2,1,0:T(2,128)(2,1)} %reshape.122), calls=%async_computation.1 | async-start | bytes 1032192 | tf_op jit(solution)/shard_map/all_to_all | solution.py:155
  257.8 0.5 select_reduce_fusion
  258.3 13.3 %all-to-all-done.1 = bf16[16,2,8064]{2,1,0:T(2,128)(2,1)} async-done(((bf16[16,2,8064]{2,1,0:T(2,128)(2,1)}), bf16[16,2,8064]{2,1,0:T(2,128)(2,1)}, u32[]{:S(2)}, u32[]{:S(2)}) %all-to-all-start.1) | async-done | bytes 516128 | tf_op jit(solution)/shard_map/all_to_all | solution.py:155
  271.6 5.0 %reshape.123 = bf16[2688,1,96]{2,1,0:T(2,128)(2,1)S(1)} reshape(bf16[16,2,8064]{2,1,0:T(2,128)(2,1)} %all-to-all-done.1) | data formatting | bytes 1032192
  276.6 2.8 copy.81
  279.4 3.3 %all_to_all.26 = bf16[1,96,16,168]{3,2,1,0:T(8,128)(2,1)S(1)} reshape(bf16[1,96,2688]{2,1,0:T(8,128)(2,1)} %copy.81) | data formatting | bytes 1032192 | tf_op jit(solution)/shard_map/all_to_all | solution.py:155
  282.7 1.2 copy.82
  283.9 0.7 reshape.116
  284.6 1.2 fusion.23
  (40 shorter events, 0.4 us)
Async XLA Ops:
  7.2 108.9 %copy-start = (bf16[256,2688]{1,0:T(8,128)(2,1)S(1)}, bf16[256,2688]{1,0:T(8,128)(2,1)}, u32[]{:S(2)}) copy-start(bf16[256,2688]{1,0:T(8,128)(2,1)} %param.33) | copy-start | bytes 4128772
  7.2 29.3 %copy-start.5 = (bf16[96,3,128]{2,0,1:T(8,128)(2,1)S(1)}, bf16[96,3,128]{2,0,1:T(8,128)(2,1)}, u32[]{:S(2)}) copy-start(bf16[96,3,128]{2,0,1:T(8,128)(2,1)} %param.26) | copy-start | bytes 221188
  7.2 165.5 %reduce-scatter.4.cloned.1.call-start = ((), (), s32[]{:S(2)}) async-start(), calls=%async_computation.3 | async-start | bytes 1462272
  7.3 47.8 %copy-start.2 = (bf16[2688,2,256]{2,1,0:T(2,128)(2,1)S(1)}, bf16[2688,2,256]{2,1,0:T(2,128)(2,1)}, u32[]{:S(2)}) copy-start(bf16[2688,2,256]{2,1,0:T(2,128)(2,1)} %param.22) | copy-start | bytes 8257540
  55.5 1.3 copy-start.7
  55.6 1.3 copy-start.4
  55.6 1.4 copy-start.10
  55.6 1.4 copy-start.9
  55.6 1.4 copy-start.11
  64.9 4.8 %copy-start.1 = (f32[96,4,64,128]{3,2,1,0:T(8,128)}, f32[96,4,64,128]{3,2,1,0:T(8,128)S(1)}, u32[]{:S(2)}) copy-start(f32[96,4,64,128]{3,2,1,0:T(8,128)S(1)} %multiply_add_fusion) | copy-start | bytes 37748740
  69.7 14.8 %copy-start.8 = (f32[4]{0:T(128)S(1)}, f32[4]{0:T(128)}, u32[]{:S(2)}) copy-start(f32[4]{0:T(128)} %param.31) | copy-start | bytes 52
  69.7 46.4 %copy-start.12 = (bf16[256]{0:T(256)(128)(2,1)S(1)}, bf16[256]{0:T(256)(128)(2,1)}, u32[]{:S(2)}) copy-start(bf16[256]{0:T(256)(128)(2,1)} %param.32) | copy-start | bytes 1540
  84.4 33.6 %copy-start.6 = (s32[96,6]{0,1:T(8,128)S(1)}, s32[96,6]{0,1:T(8,128)}, u32[]{:S(2)}) copy-start(s32[96,6]{0,1:T(8,128)} %param.37) | copy-start | bytes 6916
  84.6 88.1 %copy-start.3 = (bf16[96,168]{0,1:T(8,128)(2,1)S(1)}, bf16[96,168]{0,1:T(8,128)(2,1)}, u32[]{:S(2)}) copy-start(bf16[96,168]{0,1:T(8,128)(2,1)} %param.20) | copy-start | bytes 96772
  253.2 18.4 %all-to-all-start.1 = ((bf16[16,2,8064]{2,1,0:T(2,128)(2,1)}), bf16[16,2,8064]{2,1,0:T(2,128)(2,1)}, u32[]{:S(2)}, u32[]{:S(2)}) async-start(bf16[16,2,8064]{2,1,0:T(2,128)(2,1)} %reshape.122), calls=%async_computation.1 | async-start | bytes 1032192 | tf_op jit(solution)/shard_map/all_to_all | solution.py:155
Sparse Core Ops, SparseCore 0:
  118.0 54.5 reduce-scatter.3
where the time goes:
time: 293 us
  blocking collectives  127 us (43%)
  waiting for transfers between devices  64.1 us (22%)
  other arithmetic  29 us (10%)
  matrix products  29 us (10%)
  local copies, waits for them, and re-layouts  24.6 us (8%)
  between operations  14.5 us (5%)
  starting transfers between devices  4.53 us (2%)
    unnamed x2, waiting for transfers between devices  50.8 us
    psum x1, blocking collectives, local(): group_squares = lax.psum(partial_squares, 'wide')  31.1 us
    psum x1, blocking collectives, local(): lax.psum((jnp.sum(hidden_slice * hidden_slice, axis=1), jnp.dot(weighted,...  30.5 us
    all_gather x1, blocking collectives, local(): full_tokens = lax.all_gather(tokens, 'wide', axis=1, tiled=True)  25.6 us
    all_to_all x1, blocking collectives, local(): lax.all_to_all(sent, 'wide', split_axis=0, concat_axis=2, tiled=True)[0]  21.2 us
    all_gather x1, blocking collectives, local(): all_maps = lax.all_gather(conv_maps, 'wide', axis=1, tiled=True)  18.5 us
    unnamed x1, other arithmetic  14.9 us
    dot_general x1, matrix products, local(): jnp.einsum('shpn,sn->shp', new_state, out_maps, precision=lax.Precision.H...  14.7 us
  transfers between devices with their start and end apart: 2, of which 2 were waited for; matrix products, arithmetic and copies ran while one was open for 2% of the time, Pallas kernels for 0%

commit v1 on v0

--- a/solution.py
+++ b/solution.py
@@ -81,7 +81,8 @@
     seqs = tokens.shape[0]
     slice_width = tokens.shape[1]
     capacity = min(seqs, 4 * seqs * TOPK // devices)
-    full_tokens = lax.all_gather(tokens, "wide", axis=1, tiled=True)
+    terms = lax.all_gather(tokens, "wide", axis=0, tiled=False)
+    full_tokens = jnp.concatenate(terms, axis=1)
     tokens_float = full_tokens.astype(jnp.float32)
     normed = (tokens_float * rms_scale(tokens_float, 1) * mix_gain.astype(jnp.float32)).astype(
         jnp.bfloat16

time: 293 us -> 294 us (level)
  no operation moved by 1% of the time
where the time goes in v1:
time: 294 us; the launch traced here: 293 us
  blocking collectives  127 us (43%)
  waiting for transfers between devices  64.1 us (22%)
  other arithmetic  29.9 us (10%)
  matrix products  27.8 us (9%)
  local copies, waits for them, and re-layouts  25.4 us (9%)
  between operations  14.6 us (5%)
  starting transfers between devices  4.53 us (2%)
    unnamed x2, waiting for transfers between devices  50.8 us
    psum x1, blocking collectives, local(): group_squares = lax.psum(partial_squares, 'wide')  31.1 us
    psum x1, blocking collectives, local(): lax.psum((jnp.sum(hidden_slice * hidden_slice, axis=1), jnp.dot(weighted,...  30.5 us
    all_gather x1, blocking collectives, local(): terms = lax.all_gather(tokens, 'wide', axis=0, tiled=False)  25.6 us
    all_to_all x1, blocking collectives, local(): lax.all_to_all(sent, 'wide', split_axis=0, concat_axis=2, tiled=True)[0]  21.2 us
    all_gather x1, blocking collectives, local(): all_maps = lax.all_gather(conv_maps, 'wide', axis=1, tiled=True)  18.5 us
    unnamed x1, other arithmetic  14.9 us
    dot_general x1, matrix products, local(): jnp.einsum('shpn,sn->shp', new_state, out_maps, precision=lax.Precision.H...  14.7 us
  transfers between devices with their start and end apart: 2, of which 2 were waited for; matrix products, arithmetic and copies ran while one was open for 2% of the time, Pallas kernels for 0%

profile of v1, /device:TPU:0, one launch (start us, length us, event | category | flops | bytes accessed | tf_op | source)
XLA Modules:
  0.0 293.2 jit_solution(6500956882181372410)
XLA Ops:
  7.2 0.0 copy-start
  7.2 0.0 reduce-scatter.4.cloned.1.call-start
  7.2 0.8 convert_element_type.126
  8.0 0.8 mul.234
  8.9 25.6 %all-gather.1 = bf16[16,96,168]{1,2,0:T(8,128)(2,1)S(1)} all-gather(bf16[1,96,168]{1,2,0:T(8,128)(2,1)} %bitcast.94), channel_id=2, replica_groups=mesh['group'=2,'wide'=16] {'wide'}, dimensions={0}, use_global_device_ids=true | all-gather | bytes 548352 | tf_op jit(solution)/shard_map/all_gather | solution.py:84
  34.5 0.4 multiply_reduce_fusion
  34.9 0.7 convert_element_type.138
  35.5 0.4 fusion.12
  36.0 1.5 fusion.23
  37.5 18.5 %all_gather.11 = bf16[96,2048]{1,0:T(8,128)(2,1)S(1)} all-gather(bf16[96,128]{1,0:T(8,128)(2,1)S(1)} %multiply_convert_fusion.4), channel_id=1, replica_groups=mesh['group'=2,'wide'=16] {'wide'}, dimensions={1}, use_global_device_ids=true | all-gather | bytes 417792 | tf_op jit(solution)/shard_map/all_gather | solution.py:100
  56.0 0.4 multiply_convert_fusion
  56.5 0.0 copy-start.7
  56.5 0.5 copy.88
  57.0 0.6 convolution_convert_fusion.1
  57.7 0.1 copy.71
  57.8 0.2 multiply_exponential_fusion
  58.1 0.1 convert_multiply_fusion.1
  58.1 0.1 copy.72
  58.3 0.1 copy.70
  58.4 7.0 %multiply_add_fusion = f32[96,4,64,128]{3,2,1,0:T(8,128)S(1)} fusion(f32[96,4,64,128]{3,2,1,0:T(8,128)} %param.34, f32[96,128]{1,0:T(8,128)S(1)} %get-tuple-element.5, f32[96,4,64]{2,1,0:T(4,128)S(1)} %copy.72, f32[96,4]{1,0:T(8,128)S(1)} %copy.70), kind=kLoop, calls=%fused_computation | loop fusion | flops 9437184 | bytes 25314816 | tf_op jit(solution)/shard_map/add | solution.py:111
  65.4 0.0 copy-start.1
  65.4 4.8 %copy-done.1 = f32[96,4,64,128]{3,2,1,0:T(8,128)} copy-done((f32[96,4,64,128]{3,2,1,0:T(8,128)}, f32[96,4,64,128]{3,2,1,0:T(8,128)S(1)}, u32[]{:S(2)}) %copy-start.1) | copy-done | bytes 12582936
  70.2 14.7 %fusion.39 = f32[96,1,4,64]{3,1,2,0:T(1,128)S(1)} fusion(f32[96,4,64,128]{3,2,1,0:T(8,128)S(1)} %multiply_add_fusion, bf16[96,128,1,1]{1,0,2,3:T(8,128)(2,1)S(1)} %get-tuple-element.4), kind=kOutput, calls=%fused_computation.52 | convolution fusion | flops 37748736 | bytes 12705792 | tf_op jit(solution)/shard_map/shpn,sn->shp/dot_general | solution.py:113
  84.9 0.1 copy.84
  85.0 0.0 copy-done.8
  85.0 0.1 fusion.29
  85.1 0.1 copy.73
  85.2 0.1 multiply_reduce_fusion.3
  85.3 0.1 broadcast_multiply_fusion.1
  85.4 31.1 %psum.21 = f32[96,8]{0,1:T(8,128)S(1)} all-reduce(f32[96,8]{0,1:T(8,128)S(1)} %broadcast_multiply_fusion.1), channel_id=1, replica_groups=mesh['group'=2,'wide'=16] {'wide'}, use_global_device_ids=true, to_apply=%region_4.5 | all-reduce | flops 768 | bytes 6144 | tf_op jit(solution)/shard_map/psum | solution.py:119
  116.5 0.1 multiply_reduce_fusion.4
  116.6 1.8 fusion.38
  118.4 0.0 reduce-scatter.4.cloned.1.call-update
  118.4 0.1 copy.74
  118.5 0.1 eq.60
  118.7 1.7 reduce-window.6
  120.3 0.2 slice_reduce_fusion
  120.6 0.1 bitcast_bitcast_fusion
  120.7 0.1 reduce_sum.101
  120.9 0.1 copy.77
  120.9 0.8 dynamic-slice_convert_fusion.1
  121.7 0.6 fusion.4
  122.3 50.8 %reduce-scatter.4.cloned.1.call-done = f32[96,168]{0,1:T(8,128)} async-done(((f32[96,2688]{0,1:T(8,128)}), f32[96,168]{0,1:T(8,128)}) %reduce-scatter.4.cloned.1.call-update) | async-done | bytes 64528
  173.1 0.9 add_convert_fusion
  174.1 0.9 fusion.34
  175.0 30.5 %all-reduce.2 = (f32[96,16]{0,1:T(8,128)S(1)}, f32[96]{0:T(128)S(1)}) all-reduce(f32[96,16]{0,1:T(8,128)S(1)} %fusion.34, f32[96]{0:T(128)S(1)} %fusion.35), channel_id=1, replica_groups=mesh['group'=2,'wide'=16] {'wide'}, use_global_device_ids=true, to_apply=%region_10.11 | all-reduce | flops 1632 | bytes 13056 | tf_op jit(solution)/shard_map/psum | solution.py:135
  205.5 0.3 convolution_convert_fusion
  205.8 0.6 reshape.129
  206.4 0.2 copy.78
  206.6 21.2 %all_to_all.30 = bf16[16,96,168]{1,2,0:T(8,128)(2,1)S(1)} all-to-all(bf16[16,96,168]{1,2,0:T(8,128)(2,1)S(1)} %copy.78), channel_id=1, replica_groups=mesh['group'=2,'wide'=16] {'wide'}, dimensions={0} | all-to-all | bytes 1032192 | tf_op jit(solution)/shard_map/all_to_all | solution.py:152
  227.8 6.5 %fusion.8 = bf16[1,96,2688]{2,1,0:T(8,128)(2,1)S(1)} fusion(bf16[1,928,2688]{2,1,0:T(8,128)(2,1)} %param.39, bf16[96,2688]{0,1:T(8,128)(2,1)S(1)} %bitcast.90, bf16[1,2688,928]{1,2,0:T(8,128)(2,1)} %param.38), kind=kOutput, calls=%fused_computation.9 | convolution fusion | flops 958399488 | bytes 11010048 | tf_op jit(solution)/shard_map/dot_general | solution.py:29
  234.4 1.9 copy.80
  236.3 0.5 broadcast.131
  236.8 14.9 %reduce.4 = bf16[2688,96]{1,0:T(8,128)(2,1)S(1)} reduce(bf16[2688,1,96]{2,1,0:T(2,128)(2,1)S(1)} %bitcast.85, bf16[]{:T(256)} %broadcast.131), dimensions={1}, to_apply=%bitcast.67.reduce_sub_computation | reduce | bytes 1032194
  251.8 1.9 reshape.144
  253.7 4.5 %all-to-all-start.1 = ((bf16[16,2,8064]{2,1,0:T(2,128)(2,1)}), bf16[16,2,8064]{2,1,0:T(2,128)(2,1)}, u32[]{:S(2)}, u32[]{:S(2)}) async-start(bf16[16,2,8064]{2,1,0:T(2,128)(2,1)} %reshape.144), calls=%async_computation.1 | async-start | bytes 1032192 | tf_op jit(solution)/shard_map/all_to_all | solution.py:156
  258.3 0.5 select_reduce_fusion
  258.8 13.3 %all-to-all-done.1 = bf16[16,2,8064]{2,1,0:T(2,128)(2,1)} async-done(((bf16[16,2,8064]{2,1,0:T(2,128)(2,1)}), bf16[16,2,8064]{2,1,0:T(2,128)(2,1)}, u32[]{:S(2)}, u32[]{:S(2)}) %all-to-all-start.1) | async-done | bytes 516128 | tf_op jit(solution)/shard_map/all_to_all | solution.py:156
  272.1 5.0 %reshape.145 = bf16[2688,1,96]{2,1,0:T(2,128)(2,1)S(1)} reshape(bf16[16,2,8064]{2,1,0:T(2,128)(2,1)} %all-to-all-done.1) | data formatting | bytes 1032192
  277.1 2.8 copy.81
  279.9 3.3 %all_to_all.26 = bf16[1,96,16,168]{3,2,1,0:T(8,128)(2,1)S(1)} reshape(bf16[1,96,2688]{2,1,0:T(8,128)(2,1)} %copy.81) | data formatting | bytes 1032192 | tf_op jit(solution)/shard_map/all_to_all | solution.py:156
  283.2 1.2 copy.82
  284.4 0.7 reshape.130
  285.1 1.2 fusion.22
  (43 shorter events, 0.4 us)
Async XLA Ops:
  7.2 109.4 %copy-start = (bf16[256,2688]{1,0:T(8,128)(2,1)S(1)}, bf16[256,2688]{1,0:T(8,128)(2,1)}, u32[]{:S(2)}) copy-start(bf16[256,2688]{1,0:T(8,128)(2,1)} %param.33) | copy-start | bytes 4128772
  7.2 30.3 %copy-start.5 = (bf16[96,3,128]{2,0,1:T(8,128)(2,1)S(1)}, bf16[96,3,128]{2,0,1:T(8,128)(2,1)}, u32[]{:S(2)}) copy-start(bf16[96,3,128]{2,0,1:T(8,128)(2,1)} %param.26) | copy-start | bytes 221188
  7.2 165.9 %reduce-scatter.4.cloned.1.call-start = ((), (), s32[]{:S(2)}) async-start(), calls=%async_computation.3 | async-start | bytes 1462272
  8.9 47.6 %copy-start.2 = (bf16[2688,2,256]{2,1,0:T(2,128)(2,1)S(1)}, bf16[2688,2,256]{2,1,0:T(2,128)(2,1)}, u32[]{:S(2)}) copy-start(bf16[2688,2,256]{2,1,0:T(2,128)(2,1)} %param.22) | copy-start | bytes 8257540
  56.5 1.2 copy-start.7
  56.5 1.2 copy-start.4
  56.5 1.3 copy-start.10
  56.5 1.3 copy-start.9
  56.5 1.3 copy-start.11
  65.4 4.8 %copy-start.1 = (f32[96,4,64,128]{3,2,1,0:T(8,128)}, f32[96,4,64,128]{3,2,1,0:T(8,128)S(1)}, u32[]{:S(2)}) copy-start(f32[96,4,64,128]{3,2,1,0:T(8,128)S(1)} %multiply_add_fusion) | copy-start | bytes 37748740
  70.2 14.8 %copy-start.8 = (f32[4]{0:T(128)S(1)}, f32[4]{0:T(128)}, u32[]{:S(2)}) copy-start(f32[4]{0:T(128)} %param.31) | copy-start | bytes 52
  70.2 46.4 %copy-start.12 = (bf16[256]{0:T(256)(128)(2,1)S(1)}, bf16[256]{0:T(256)(128)(2,1)}, u32[]{:S(2)}) copy-start(bf16[256]{0:T(256)(128)(2,1)} %param.32) | copy-start | bytes 1540
  84.8 33.5 %copy-start.6 = (s32[96,6]{0,1:T(8,128)S(1)}, s32[96,6]{0,1:T(8,128)}, u32[]{:S(2)}) copy-start(s32[96,6]{0,1:T(8,128)} %param.37) | copy-start | bytes 6916
  84.9 88.3 %copy-start.3 = (bf16[96,168]{0,1:T(8,128)(2,1)S(1)}, bf16[96,168]{0,1:T(8,128)(2,1)}, u32[]{:S(2)}) copy-start(bf16[96,168]{0,1:T(8,128)(2,1)} %param.20) | copy-start | bytes 96772
  253.7 18.4 %all-to-all-start.1 = ((bf16[16,2,8064]{2,1,0:T(2,128)(2,1)}), bf16[16,2,8064]{2,1,0:T(2,128)(2,1)}, u32[]{:S(2)}, u32[]{:S(2)}) async-start(bf16[16,2,8064]{2,1,0:T(2,128)(2,1)} %reshape.144), calls=%async_computation.1 | async-start | bytes 1032192 | tf_op jit(solution)/shard_map/all_to_all | solution.py:156
Sparse Core Ops, SparseCore 0:
  118.5 54.5 reduce-scatter.3
